TPU v7x, 128 devices: a whole 4x4x4 slice. The times are simulated.
128 devices in a mesh: req: 4 (over y), tok: 32 (over z, x, core).
Axes of the slice: x: 4, y: 4, z: 4, core: 2. Of those that a mesh axis runs over, the one named last changes fastest.
Arguments:
- tokens: bfloat16 [8, 2048, 1536], P('req', 'tok'), may hold values from -16 to 16
- gain_attn: float32 [1536], replicated, may hold values from 0.1 to 1.9
- query_weight: bfloat16 [1536, 1536], replicated, may hold values from -0.375 to 0.375
- key_value_weight: bfloat16 [1536, 1024], replicated, may hold values from -0.15625 to 0.15625
- w_out: bfloat16 [1536, 1536], replicated, may hold values from -0.15625 to 0.15625
- kv_pool: bfloat16 [512, 64, 1024], P(('req', 'tok')), may hold values from -170 to 170, as said below
- migrate: int32 [512], P(('req', 'tok')), may hold values from 0 to 511, as said below
- page_table: int32 [8, 64], P('req'), may hold values from 0 to 127, as said below
- cache_len: int32 [8], P('req'), may hold values from 0 to 4096, as said below
- gain_ffn: float32 [1536], replicated, may hold values from 0.1 to 1.9
- routes: int32 [8, 2048, 8], P('req', 'tok'), may hold values from 0 to 31, all different within a row; in each aligned block of 64 rows (0 to 63, 64 to 127, ..., all dimensions but the last counted through in order) at most 24 rows name the same one
- gate_weights: float32 [8, 2048, 8], P('req', 'tok'), may hold values from 0.05 to 0.5
- w_gate_up: bfloat16 [32, 1536, 1024], P('tok'), may hold values from -0.15625 to 0.15625
- w_down: bfloat16 [32, 512, 1536], P('tok'), may hold values from -0.25 to 0.25
Outputs:
- attended: bfloat16 [8, 2048, 1536], P('req', 'tok')
- expert_mix: bfloat16 [8, 2048, 1536], P('req', 'tok')
Inputs may be any that keep to these rules, and one draw needn't show every extreme that they name: `kv_pool`: the values of the cached keys and values. `migrate`: A permutation of all slots that keeps a slot's tok index: slot a*128 + t*4 + i goes to some a2*128 + t*4 + i2. `page_table`: the rows of the 2 requests of one group together hold every slot of the group's pool exactly once. `cache_len`: each length lies within 128 of 0 or of 4096; some request has exactly 4096. `routes`: the 8 experts of a token differ; in each aligned block of 64 rows (one request's tokens on one device) no expert is named more than 24 times.
All inputs are finite; a program needn't handle non-finite values.
Results may differ from a plain program's by a relative error of at most 0.025.
Values may be sent and summed in bfloat16 or wider, within the bound.
No kernel may reach another device: no remote copies, remote signals or barrier semaphores. Data moves between devices by JAX's collectives and lax.ppermute only.
A program may use at most 192 MiB of HBM per device.

v0:
```python
import jax
import jax.numpy as jnp
from jax import lax
from jax.sharding import PartitionSpec as P

QUERY_HEADS = 24
KEY_VALUE_HEADS = 8
HEAD_SIZE = 64
FF = 512
TOPK = 8
MOST = 24
score_masked = -1e30
epsilon = 1e-06
far_position = 1 << 30


def rms_norm(values, gain_vec):
    widened = values.astype(jnp.float32)
    inverse = lax.rsqrt(jnp.mean(widened * widened, axis=-1, keepdims=True) + epsilon)
    return (widened * inverse * gain_vec).astype(jnp.bfloat16)


def pick_block(row_total):
    block_len = min(row_total, 1024)
    while row_total % block_len:
        block_len -= 1
    return block_len


def attend(running, head_rows, meta_abs, query_heads, query_abs):
    row_total = head_rows.shape[1]
    block_len = pick_block(row_total)
    blocks = row_total // block_len
    heads_kv = query_heads.shape[0]
    head_dim = query_heads.shape[2]

    def loop_step(index, carried):
        run_max, run_sum, run_acc = carried
        block = lax.dynamic_slice_in_dim(head_rows, index * block_len, block_len, 1)
        abs_block = lax.dynamic_slice_in_dim(meta_abs, index * block_len, block_len, 0)
        visible = (abs_block[None, :] <= query_abs[:, None])[None, :, :]
        scores = jnp.einsum(
            "hqd,hkd->hqk", query_heads, block[:heads_kv], preferred_element_type=jnp.float32
        ) * head_dim ** (-0.5)
        scores = jnp.where(visible, scores, score_masked)
        new_max = jnp.maximum(run_max, jnp.max(scores, axis=-1))
        weight = jnp.where(visible, jnp.exp(scores - new_max[..., None]), 0.0)
        factor = jnp.exp(run_max - new_max)
        run_sum = run_sum * factor + jnp.sum(weight, axis=-1)
        update = jnp.einsum(
            "hqk,hkd->hqd",
            weight.astype(jnp.bfloat16),
            block[heads_kv:],
            preferred_element_type=jnp.float32,
        )
        run_acc = run_acc * factor[..., None] + update
        return (new_max, run_sum, run_acc)

    return lax.fori_loop(0, blocks, loop_step, running)


def pick_member(state, member_id):
    return jax.tree.map(lambda array: array[member_id], state)


def stack_members(states):
    return jax.tree.map(lambda *arrays: jnp.stack(arrays), *states)


def local(
    tokens,
    gain_attn,
    query_weight,
    key_value_weight,
    w_out,
    kv_pool,
    migrate,
    page_table,
    cache_len,
    gain_ffn,
    routes,
    gate_weights,
    w_gate_up,
    w_down,
):
    request_per_shard, tokens_per_shard, model_width = tokens.shape
    local_rows = request_per_shard * tokens_per_shard
    tok_count = lax.axis_size("tok")
    req_count = lax.axis_size("req")
    tok_index = lax.axis_index("tok")
    kv_width = key_value_weight.shape[1]
    groups_per_head = QUERY_HEADS // KEY_VALUE_HEADS
    flat_rows = tokens.reshape(local_rows, model_width)
    normalized_input = rms_norm(flat_rows, gain_attn)
    query_rows = (
        jnp.dot(normalized_input, query_weight, preferred_element_type=jnp.float32)
        .astype(jnp.bfloat16)
        .reshape(request_per_shard, tokens_per_shard, KEY_VALUE_HEADS, groups_per_head, HEAD_SIZE)
    )
    query_heads = query_rows.transpose(0, 2, 3, 1, 4).reshape(
        request_per_shard, KEY_VALUE_HEADS, groups_per_head * tokens_per_shard, HEAD_SIZE
    )
    keyval_pos = (
        jnp.einsum(
            "rcd,dk->crk",
            normalized_input.reshape(request_per_shard, tokens_per_shard, model_width),
            key_value_weight,
            preferred_element_type=jnp.float32,
        )
        .astype(jnp.bfloat16)
        .reshape(tokens_per_shard, request_per_shard * kv_width)
    )
    span_pos = jnp.arange(tokens_per_shard, dtype=jnp.int32)
    query_abs = cache_len[:, None] + tok_index * tokens_per_shard + span_pos[None, :]
    query_abs_rep = jnp.tile(query_abs, (1, groups_per_head))
    pages_dev = kv_pool.shape[0]
    page_rows = kv_pool.shape[1]
    pages_req = page_table.shape[1]
    slots_all = request_per_shard * pages_req
    cache_pos = jnp.arange(pages_req * page_rows, dtype=jnp.int32)
    target = migrate // slots_all * pages_dev + migrate % pages_dev
    places = jnp.arange(req_count * pages_dev, dtype=jnp.int32)
    route_pages = (places[:, None] == target[None, :]).astype(jnp.bfloat16)
    outgoing = jnp.einsum(
        "sp,prk->srk", route_pages, kv_pool, preferred_element_type=jnp.float32
    ).astype(jnp.bfloat16)
    outgoing = outgoing.reshape(req_count, pages_dev, page_rows, kv_width)
    arrived = lax.all_to_all(outgoing, "req", split_axis=0, concat_axis=0, tiled=True)
    migrated = jnp.sum(arrived, axis=0, dtype=jnp.float32).astype(jnp.bfloat16)
    query_count = groups_per_head * tokens_per_shard
    start_state = (
        jnp.full((request_per_shard, KEY_VALUE_HEADS, query_count), score_masked, jnp.float32),
        jnp.zeros((request_per_shard, KEY_VALUE_HEADS, query_count), jnp.float32),
        jnp.zeros((request_per_shard, KEY_VALUE_HEADS, query_count, HEAD_SIZE), jnp.float32),
    )
    pool_all = lax.all_gather(migrated, "tok", axis=0, tiled=True)
    pool_heads = pool_all.reshape(
        pool_all.shape[0], page_rows, 2 * KEY_VALUE_HEADS, HEAD_SIZE
    ).transpose(2, 0, 1, 3)
    results = []
    for member_id in range(request_per_shard):
        rows = jnp.take(pool_heads, page_table[member_id], axis=1).reshape(
            2 * KEY_VALUE_HEADS, pages_req * page_rows, HEAD_SIZE
        )
        cache_abs = jnp.where(cache_pos < cache_len[member_id], cache_pos, far_position)
        results.append(
            attend(
                pick_member(start_state, member_id),
                rows,
                cache_abs,
                query_heads[member_id],
                query_abs_rep[member_id],
            )
        )
    running = stack_members(results)
    piece = lax.all_gather(keyval_pos, "tok", axis=0, tiled=True)
    row_total = piece.shape[0]
    by_member = piece.reshape(
        row_total, request_per_shard, 2 * KEY_VALUE_HEADS, HEAD_SIZE
    ).transpose(1, 2, 0, 3)
    positions = jnp.arange(row_total, dtype=jnp.int32)
    fold_results = []
    for member_id in range(request_per_shard):
        piece_abs = cache_len[member_id] + positions
        fold_results.append(
            attend(
                pick_member(running, member_id),
                by_member[member_id],
                piece_abs,
                query_heads[member_id],
                query_abs_rep[member_id],
            )
        )
    final_state = stack_members(fold_results)
    run_max, run_sum, run_acc = final_state
    normalized_heads = (
        (run_acc / run_sum[..., None])
        .astype(jnp.bfloat16)
        .reshape(request_per_shard, KEY_VALUE_HEADS, groups_per_head, tokens_per_shard, HEAD_SIZE)
    )
    heads_out = normalized_heads.transpose(0, 3, 1, 2, 4).reshape(
        local_rows, QUERY_HEADS * HEAD_SIZE
    )
    projected = jnp.dot(heads_out, w_out, preferred_element_type=jnp.float32)
    attended = projected.astype(jnp.bfloat16)
    residual = (flat_rows.astype(jnp.float32) + projected).astype(jnp.bfloat16)
    normed_ffn = rms_norm(residual, gain_ffn)
    member = jnp.arange(request_per_shard, dtype=jnp.int32)
    experts_total = tok_count * w_gate_up.shape[0]
    route_local = routes.reshape(request_per_shard, tokens_per_shard * TOPK)
    onehot = route_local[..., None] == jnp.arange(experts_total, dtype=jnp.int32)[None, None, :]
    rank_all = jnp.cumsum(onehot.astype(jnp.int32), axis=1) - 1
    rank_of = jnp.sum(jnp.where(onehot, rank_all, 0), axis=2)
    slot_of = route_local * (request_per_shard * MOST) + member[:, None] * MOST + rank_of
    slot_flat = slot_of.reshape(-1)
    capacity = experts_total * request_per_shard * MOST
    token_ids = jnp.arange(local_rows * TOPK, dtype=jnp.int32) // TOPK
    source = jnp.zeros((capacity,), jnp.int32).at[slot_flat].set(token_ids + 1)
    gathered = jnp.take(normed_ffn, jnp.maximum(source - 1, 0), axis=0)
    outbound = jnp.where((source > 0)[:, None], gathered, jnp.zeros_like(gathered)).reshape(
        experts_total, request_per_shard * MOST, model_width
    )
    inbound = lax.all_to_all(outbound, "tok", split_axis=0, concat_axis=1, tiled=True)
    gate_up = jnp.einsum("erd,edf->erf", inbound, w_gate_up, preferred_element_type=jnp.float32)
    hidden = (jax.nn.silu(gate_up[..., :FF]) * gate_up[..., FF:]).astype(jnp.bfloat16)
    expert_out = jnp.einsum(
        "erf,efd->erd", hidden, w_down, preferred_element_type=jnp.float32
    ).astype(jnp.bfloat16)
    returned = lax.all_to_all(expert_out, "tok", split_axis=1, concat_axis=0, tiled=True)
    picked = jnp.take(returned.reshape(capacity, model_width), slot_flat, axis=0).reshape(
        local_rows, TOPK, model_width
    )
    mixture = jnp.einsum(
        "qk,qkd->qd", gate_weights.reshape(local_rows, TOPK), picked.astype(jnp.float32)
    )
    return (
        attended.reshape(request_per_shard, tokens_per_shard, model_width),
        mixture.astype(jnp.bfloat16).reshape(request_per_shard, tokens_per_shard, model_width),
    )


def solution(mesh):
    placed = (
        P("req", "tok", None),
        P(),
        P(),
        P(),
        P(),
        P(("req", "tok"), None, None),
        P(("req", "tok")),
        P("req", None),
        P("req"),
        P(),
        P("req", "tok", None),
        P("req", "tok", None),
        P("tok", None, None),
        P("tok", None, None),
    )
    return jax.shard_map(
        local,
        mesh=mesh,
        in_specs=placed,
        out_specs=(P("req", "tok", None), P("req", "tok", None)),
        check_vma=False,
    )
```

profile of v0, /device:TPU:0, one launch (start us, length us, event | category | flops | bytes accessed | tf_op | source)
XLA Modules:
  0.0 831.7 jit_solution(13190696790973247134)
XLA Ops:
  21.8 30.8 %all_to_all.23 = bf16[4,4,64,1024]{3,1,2,0:T(4,128)(2,1)} all-to-all(bf16[4,4,64,1024]{3,1,2,0:T(4,128)(2,1)S(1)} %copy.95), channel_id=1, replica_groups=mesh['req'=4,'tok'=32] {'req'}, dimensions={0} | all-to-all | bytes 4194304 | tf_op jit(solution)/shard_map/all_to_all | solution.py:128
  101.6 12.4 %copy.105 = bf16[2048,2048]{0,1:T(8,128)(2,1)} copy(bf16[2048,2048]{1,0:T(8,128)(2,1)} %all-gather.5.cloned.1.call-done) | data formatting | bytes 16777216 | tf_op jit(solution)/shard_map/all_gather | solution.py:156
  114.0 6.4 slice_bitcast_fusion.1
  120.4 21.6 %all-gather.3.cloned.1.call-done = bf16[128,64,1024]{2,1,0:T(8,128)(2,1)} async-done(((bf16[4,64,1024]{2,1,0:T(8,128)(2,1)}), bf16[128,64,1024]{2,1,0:T(8,128)(2,1)}) %all-gather.3.cloned.1.call-update) | async-done | bytes 16777232 | tf_op jit(solution)/shard_map/all_gather | solution.py:136
  142.0 23.0 %copy.98 = bf16[128,64,1024]{0,2,1:T(8,128)(2,1)} copy(bf16[128,64,1024]{2,1,0:T(8,128)(2,1)} %all-gather.3.cloned.1.call-done) | data formatting | bytes 33554432 | tf_op jit(solution)/shard_map/all_gather | solution.py:136
  165.1 46.1 %copy.99 = bf16[128,64,16,64]{3,1,0,2:T(8,128)(2,1)} copy(bf16[128,64,16,64]{0,3,2,1:T(8,128)(2,1)} %bitcast.228) | data formatting | bytes 33554432 | tf_op jit(solution)/shard_map/reshape | solution.py:137
  211.1 11.9 %gather_fusion.2 = bf16[64,16,64,64]{3,2,1,0:T(8,128)(2,1)} fusion(bf16[16,128,64,64]{3,2,1,0:T(8,128)(2,1)} %bitcast.226, s32[1024]{0:T(1024)S(1)} %pad_clamp_fusion.2), kind=kCustom, calls=%fused_computation.clone | custom fusion | bytes 16777472 | tf_op jit(solution)/shard_map/jit(_take)/gather | solution.py:142
  223.0 11.9 %gather_fusion.3 = bf16[64,16,64,64]{3,2,1,0:T(8,128)(2,1)} fusion(bf16[16,128,64,64]{3,2,1,0:T(8,128)(2,1)} %bitcast.227, s32[1024]{0:T(1024)S(1)} %pad_clamp_fusion.1), kind=kCustom, calls=%fused_computation.1.clone | custom fusion | bytes 16777472 | tf_op jit(solution)/shard_map/jit(_take)/gather | solution.py:142
  234.9 23.0 %select_bitcast_fusion = (bf16[16,64,64,64]{3,2,0,1:T(8,128)(2,1)}, bf16[16,64,64,64]{3,2,0,1:T(8,128)(2,1)}) fusion(bf16[64,16,64,64]{3,2,1,0:T(8,128)(2,1)} %gather_fusion.3, pred[64]{0:T(512)(128)(4,1)S(1)} %get-tuple-element.895, bf16[64,16,64,64]{3,2,1,0:T(8,128)(2,1)} %gather_fusion.2, pred[64]{0:T(512)(128)(4,1)S(1)} %get-tuple-element.873), kind=kLoop, calls=%fused_computation.91 | loop fusion | flops 8388608 | bytes 33554560 | tf_op jit(solution)/shard_map/jit(_take)/select_n | solution.py:142
  257.9 22.9 %copy.100 = bf16[16,64,64,64]{2,1,3,0:T(8,128)(2,1)} copy(bf16[16,64,64,64]{3,2,0,1:T(8,128)(2,1)} %get-tuple-element.902) | data formatting | bytes 16777216 | tf_op jit(solution)/shard_map/jit(_take)/select_n | solution.py:142
  280.7 22.6 %reshape.410 = bf16[16,4096,64]{1,2,0:T(8,128)(2,1)} reshape(bf16[16,64,64,64]{2,1,3,0:T(8,128)(2,1)} %copy.100) | data formatting | bytes 16777216 | tf_op jit(solution)/shard_map/reshape | solution.py:142
  303.3 60.5 %while.74 = (s32[]{:T(128)}, f32[8,192]{1,0:T(8,128)S(1)}, f32[8,192]{1,0:T(8,128)S(1)}, f32[8,192,64]{1,2,0:T(8,128)}, s32[4096]{0:T(1024)S(1)}, /*index=5*/bf1...) while((s32[]{:T(128)}, f32[8,192]{1,0:T(8,128)S(1)}, ...), condition=%wide.region_5.7_spmd.clone, body=%wide.region_2.6_spmd.clone.sunk | while | flops 423599616 | bytes 24100308 | solution.py:59
  303.6 5.2 fusion.178
  312.8 5.6 fusion.181
  318.6 5.2 fusion.178
  327.8 5.7 fusion.181
  333.8 5.2 fusion.178
  343.0 5.7 fusion.181
  349.0 5.2 fusion.178
  358.1 5.7 fusion.181
  363.9 27.0 %while.72 = (s32[]{:T(128)}, f32[8,192]{1,0:T(8,128)S(1)}, f32[8,192]{1,0:T(8,128)S(1)}, f32[8,192,64]{1,2,0:T(8,128)}, s32[2048]{0:T(1024)S(1)}, /*index=5*/bf1...) while((s32[]{:T(128)}, f32[8,192]{1,0:T(8,128)S(1)}, ...), condition=%wide.region_9.11_spmd.clone, body=%wide.region_6.10_spmd.clone.sunk | while | flops 423496704 | bytes 49266148 | solution.py:59
  371.8 5.7 fusion.168
  385.1 5.7 fusion.168
  391.5 22.9 %copy.108 = bf16[16,64,64,64]{2,1,3,0:T(8,128)(2,1)} copy(bf16[16,64,64,64]{3,2,0,1:T(8,128)(2,1)} %get-tuple-element.901) | data formatting | bytes 16777216 | tf_op jit(solution)/shard_map/jit(_take)/select_n | solution.py:142
  414.4 22.6 %reshape.414 = bf16[16,4096,64]{1,2,0:T(8,128)(2,1)} reshape(bf16[16,64,64,64]{2,1,3,0:T(8,128)(2,1)} %copy.108) | data formatting | bytes 16777216 | tf_op jit(solution)/shard_map/reshape | solution.py:142
  437.0 63.0 %while.75 = (s32[]{:T(128)}, f32[8,192]{1,0:T(8,128)S(1)}, f32[8,192]{1,0:T(8,128)S(1)}, f32[8,192,64]{1,2,0:T(8,128)}, s32[4096]{0:T(1024)}, /*index=5*/bf16[16...) while((s32[]{:T(128)}, f32[8,192]{1,0:T(8,128)S(1)}, ...), condition=%wide.region_13.15_spmd.clone, body=%wide.region_10.14_spmd.clone.sunk | while | flops 423599616 | bytes 24100308 | solution.py:59
  438.0 5.2 fusion.185
  447.1 5.6 fusion.188
  453.6 5.2 fusion.185
  462.7 5.7 fusion.188
  469.4 5.2 fusion.185
  478.5 5.7 fusion.188
  485.2 5.2 fusion.185
  494.3 5.7 fusion.188
  500.0 27.1 %while.73 = (s32[]{:T(128)}, f32[8,192]{1,0:T(8,128)S(1)}, f32[8,192]{1,0:T(8,128)S(1)}, f32[8,192,64]{1,2,0:T(8,128)}, s32[2048]{0:T(1024)S(1)}, /*index=5*/bf1...) while((s32[]{:T(128)}, f32[8,192]{1,0:T(8,128)S(1)}, ...), condition=%wide.region_17.19_spmd.clone, body=%wide.region_14.18_spmd.clone.sunk | while | flops 423496704 | bytes 49266148 | solution.py:59
  508.1 5.7 fusion.174
  521.5 5.7 fusion.174
  545.9 6.2 gather_fusion
  554.9 62.1 %all_to_all.24 = bf16[32,48,1536]{2,1,0:T(8,128)(2,1)S(1)} all-to-all(bf16[32,48,1536]{2,1,0:T(8,128)(2,1)S(1)} %select_select_fusion), channel_id=1, replica_groups=mesh['req'=4,'tok'=32] {'tok'}, dimensions={0} | all-to-all | bytes 9437184 | tf_op jit(solution)/shard_map/all_to_all | solution.py:203
  617.0 5.4 convolution_bitcast_fusion
  625.3 52.2 %copy.141 = bf16[1,1536,1536]{2,0,1:T(2,128)(2,1)} copy(bf16[1,1536,1536]{2,1,0:T(8,128)(2,1)S(1)} %fusion.78) | data formatting | bytes 9437184 | tf_op jit(solution)/shard_map/convert_element_type | solution.py:208
  678.1 32.0 %reduce.4 = bf16[1536,1536]{1,0:T(8,128)(2,1)} reduce(bf16[1536,1,1536]{2,1,0:T(2,128)(2,1)} %bitcast.229, bf16[]{:T(256)} %broadcast.485), dimensions={1}, to_apply=%bitcast.192.reduce_sub_computation | reduce | bytes 9437186
  710.0 8.2 reshape.485
  718.3 5.2 all-to-all-start.2
  724.2 59.0 %all-to-all-done.2 = bf16[32,2,36864]{2,1,0:T(2,128)(2,1)} async-done(((bf16[32,2,36864]{2,1,0:T(2,128)(2,1)}), bf16[32,2,36864]{2,1,0:T(2,128)(2,1)}, u32[]{:S(2)}, u32[]{:S(2)}) %all-to-all-start.2) | async-done | bytes 4718624 | tf_op jit(solution)/shard_map/all_to_all | solution.py:209
  783.2 20.2 %reshape.486 = bf16[1536,1,1536]{2,1,0:T(2,128)(2,1)} reshape(bf16[32,2,36864]{2,1,0:T(2,128)(2,1)} %all-to-all-done.2) | data formatting | bytes 9437184
  803.4 7.2 copy.139
  810.7 10.2 %gather_fusion.1 = bf16[1024,1536]{1,0:T(8,128)(2,1)} fusion(bf16[1536,1536]{1,0:T(8,128)(2,1)} %bitcast.225, s32[1024]{0:T(1024)S(1)} %broadcast_clamp_fusion), kind=kCustom, calls=%fused_computation.3 | custom fusion | bytes 6295552 | tf_op jit(solution)/shard_map/jit(_take)/gather | solution.py:210
  (246 shorter events, 160.3 us)
Async XLA Ops:
  7.2 609.8 %copy-start = (bf16[1,1536,1024]{2,1,0:T(8,128)(2,1)S(1)}, bf16[1,1536,1024]{2,1,0:T(8,128)(2,1)}, u32[]{:S(2)}) copy-start(bf16[1,1536,1024]{2,1,0:T(8,128)(2,1)} %param.36) | copy-start | bytes 9437188
  7.2 4.8 copy-start.24
  7.2 94.4 %all-gather.5.cloned.1.call-start = ((), (), s32[]{:S(2)}) async-start(), calls=%async_computation.4 | async-start | bytes 8650752 | tf_op jit(solution)/shard_map/all_gather | solution.py:156
  12.0 130.0 %all-gather.3.cloned.1.call-start = ((), (), s32[]{:S(2)}) async-start(), calls=%async_computation.3 | async-start | bytes 17301504 | tf_op jit(solution)/shard_map/all_gather | solution.py:136
  19.4 44.1 %copy-start.3 = (bf16[2,64,1536]{2,1,0:T(8,128)(2,1)S(1)}, bf16[2,64,1536]{2,1,0:T(8,128)(2,1)}, u32[]{:S(2)}) copy-start(bf16[2,64,1536]{2,1,0:T(8,128)(2,1)} %param.24) | copy-start | bytes 1179652
  86.4 27.6 %copy-start.12 = (s32[2,512]{1,0:T(2,128)}, s32[2,512]{1,0:T(2,128)S(1)}, u32[]{:S(2)}) copy-start(s32[2,512]{1,0:T(2,128)S(1)} %fusion.111) | copy-start | bytes 12292
  87.2 26.9 %copy-start.9 = (s32[2,64,8]{1,2,0:T(8,128)}, s32[2,64,8]{1,2,0:T(8,128)S(1)}, u32[]{:S(2)}) copy-start(s32[2,64,8]{1,2,0:T(8,128)S(1)} %broadcast_multiply_fusion) | copy-start | bytes 12292
  87.4 0.6 copy-start.21
  88.0 26.0 %copy-start.17 = (s32[1024,1]{0,1:T(1,128)}, s32[1024,1]{0,1:T(1,128)S(1)}, u32[]{:S(2)}) copy-start(s32[1024,1]{0,1:T(1,128)S(1)} %compare_select_fusion) | copy-start | bytes 12292
  367.0 2.7 copy-start.1
  380.4 2.7 copy-start.1
  414.4 22.6 %copy-start.6 = (f32[8,192]{1,0:T(8,128)S(1)}, f32[8,192]{1,0:T(8,128)}, u32[]{:S(2)}) copy-start(f32[8,192]{1,0:T(8,128)} %custom-call.3) | copy-start | bytes 18436
  414.4 22.6 %copy-start.7 = (f32[8,192]{1,0:T(8,128)S(1)}, f32[8,192]{1,0:T(8,128)}, u32[]{:S(2)}) copy-start(f32[8,192]{1,0:T(8,128)} %custom-call.4) | copy-start | bytes 18436
  414.4 22.6 %copy-start.11 = (s32[64]{0:T(128)S(1)}, s32[64]{0:T(128)}, u32[]{:S(2)}) copy-start(s32[64]{0:T(128)} %get-tuple-element.1177) | copy-start | bytes 772
  437.0 63.0 %copy-start.8 = (s32[2048]{0:T(1024)S(1)}, s32[2048]{0:T(1024)}, u32[]{:S(2)}) copy-start(s32[2048]{0:T(1024)} %iota_add_fusion) | copy-start | bytes 24580
  503.3 2.7 copy-start.2
  516.7 2.7 copy-start.2
  527.1 14.4 %copy-start.4 = (bf16[2,64,1536]{2,1,0:T(8,128)(2,1)S(1)}, bf16[2,64,1536]{2,1,0:T(8,128)(2,1)}, u32[]{:S(2)}) copy-start(bf16[2,64,1536]{2,1,0:T(8,128)(2,1)} %param.24) | copy-start | bytes 1179652
  530.0 15.0 %copy-start.19 = (f32[1536]{0:T(1024)S(1)}, f32[1536]{0:T(1024)}, u32[]{:S(2)}) copy-start(f32[1536]{0:T(1024)} %param.33) | copy-start | bytes 18436
  533.0 12.9 %copy-start.14 = (s32[2048]{0:T(1024)S(1)}, s32[2048]{0:T(1024)}, u32[]{:S(2)}) copy-start(s32[2048]{0:T(1024)} %pad_clamp_fusion) | copy-start | bytes 24580
  541.6 3.4 copy-start.5
  545.9 6.2 copy-start.15
  545.9 6.2 copy-start.16
  617.0 5.4 copy-start.23
  718.3 5.2 copy-start.13
  718.3 5.4 copy-start.10
  718.3 5.5 copy-start.22
  718.3 5.8 copy-start.20
  718.3 5.9 copy-start.18
  718.3 64.9 %all-to-all-start.2 = ((bf16[32,2,36864]{2,1,0:T(2,128)(2,1)}), bf16[32,2,36864]{2,1,0:T(2,128)(2,1)}, u32[]{:S(2)}, u32[]{:S(2)}) async-start(bf16[32,2,36864]{2,1,0:T(2,128)(2,1)} %reshape.485), calls=%async_computation.2 | async-start | bytes 9437184 | tf_op jit(solution)/shard_map/all_to_all | solution.py:209
Sparse Core Ops, SparseCore 0:
  12.1 55.4 all-gather.4
  69.9 72.0 all-gather.2
where the time goes:
time: 845 us; the launch traced here: 832 us
  local copies, waits for them, and re-layouts  372 us (44%)
  matrix products  145 us (17%)
  other arithmetic  120 us (14%)
  blocking collectives  92.9 us (11%)
  waiting for transfers between devices  80.6 us (10%)
  between operations  14.7 us (2%)
    dot_general x12, matrix products, loop_step(): jnp.einsum('hqk,hkd->hqd', weight.astype(jnp.bfloat16), block[heads_kv:],...  68.1 us
    all_to_all x1, blocking collectives, local(): lax.all_to_all(outbound, 'tok', split_axis=0, concat_axis=1, tiled=True)  62.1 us
    all_to_all x1, waiting for transfers between devices, local(): lax.all_to_all(expert_out, 'tok', split_axis=1, concat_axis=0, tiled=True)  59 us
    convert_element_type x1, local copies, waits for them, and re-layouts, local(): expert_out = jnp.einsum('erf,efd->erd', hidden, w_down, preferred_element...  52.2 us
    dot_general x12, matrix products, loop_step(): jnp.einsum('hqd,hkd->hqk', query_heads, block[:heads_kv], preferred_eleme...  52.2 us
    reshape x1, local copies, waits for them, and re-layouts, local(): pool_all.reshape(pool_all.shape[0], page_rows, 2 * KEY_VALUE_HEADS, HEAD_...  46.1 us
    select_n x2, local copies, waits for them, and re-layouts, local(): jnp.take(pool_heads, page_table[member_id], axis=1)  45.8 us
    reshape x2, local copies, waits for them, and re-layouts, local(): jnp.take(pool_heads, page_table[member_id], axis=1)  45.2 us
  transfers between devices with their start and end apart: 3, of which 2 were waited for; matrix products, arithmetic and copies ran while one was open for 9% of the time, Pallas kernels for 0%

commit v1 on v0

--- a/solution.py
+++ b/solution.py
@@ -133,7 +133,15 @@
         jnp.zeros((request_per_shard, KEY_VALUE_HEADS, query_count), jnp.float32),
         jnp.zeros((request_per_shard, KEY_VALUE_HEADS, query_count, HEAD_SIZE), jnp.float32),
     )
-    pool_all = lax.all_gather(migrated, "tok", axis=0, tiled=True)
+    pool_all = jnp.concatenate(
+        lax.all_to_all(
+            jnp.stack([migrated for _ in range(lax.axis_size("tok"))], axis=0),
+            split_axis=0,
+            axis_name="tok",
+            concat_axis=0,
+        ),
+        axis=0,
+    )
     pool_heads = pool_all.reshape(
         pool_all.shape[0], page_rows, 2 * KEY_VALUE_HEADS, HEAD_SIZE
     ).transpose(2, 0, 1, 3)

time: 845 us -> 988 us (1.17)
  waiting for transfers between devices: 80.6 us -> 241 us
  blocking collectives: 92.9 us -> 59.9 us
  starting transfers between devices: 5.29 us -> 18.1 us
    all_to_all x0 -> x2, waiting for transfers between devices: none -> 167 us  [the longest x1 144 us: local(): lax.all_to_all(jnp.stack([migrated for _ in range(lax.axis_size('tok'))],...]
    another operation x2 -> x5, local copies, waits for them, and re-layouts: 0.32 us -> 72.7 us  [the longest x2 66.2 us: local(): pool_all.reshape(pool_all.shape[0], page_rows, 2 * KEY_VALUE_HEADS, HEAD_...]
    reshape x1 -> x0, local copies, waits for them, and re-layouts: 46.1 us -> none  [local(): pool_all.reshape(pool_all.shape[0], page_rows, 2 * KEY_VALUE_HEADS, HEAD_...]
    all_to_all x1 -> x0, blocking collectives: 30.8 us -> none  [local(): lax.all_to_all(outgoing, 'req', split_axis=0, concat_axis=0, tiled=True)]
    all_gather x1 -> x0, local copies, waits for them, and re-layouts: 23 us -> none  [local(): pool_all = lax.all_gather(migrated, 'tok', axis=0, tiled=True)]
    all_gather x1 -> x0, waiting for transfers between devices: 21.6 us -> none  [local(): pool_all = lax.all_gather(migrated, 'tok', axis=0, tiled=True)]
    all_gather x1, waiting for transfers between devices: 0.01 us -> 14.1 us  [local(): piece = lax.all_gather(keyval_pos, 'tok', axis=0, tiled=True)]
    all_to_all x0 -> x2, starting transfers between devices: none -> 12.9 us  [the longest x1 8.34 us: local(): lax.all_to_all(jnp.stack([migrated for _ in range(lax.axis_size('tok'))],...]
  transfers between devices with their start and end apart: 3 -> 4, of which waited for: 2 -> 4; matrix products, arithmetic and copies ran while one was open for 9% -> 8% of each run, Pallas kernels for 0% -> 0%
where the time goes in v1:
time: 988 us; the launch traced here: 975 us
  local copies, waits for them, and re-layouts  375 us (38%)
  waiting for transfers between devices  241 us (24%)
  matrix products  145 us (15%)
  other arithmetic  121 us (12%)
  blocking collectives  59.9 us (6%)
  starting transfers between devices  18.1 us (2%)
  between operations  14.6 us (1%)
    all_to_all x1, waiting for transfers between devices, local(): lax.all_to_all(jnp.stack([migrated for _ in range(lax.axis_size('tok'))],...  144 us
    dot_general x12, matrix products, loop_step(): jnp.einsum('hqk,hkd->hqd', weight.astype(jnp.bfloat16), block[heads_kv:],...  68 us
    another operation x2, local copies, waits for them, and re-layouts, local(): pool_all.reshape(pool_all.shape[0], page_rows, 2 * KEY_VALUE_HEADS, HEAD_...  66.2 us
    all_to_all x1, blocking collectives, local(): lax.all_to_all(outbound, 'tok', split_axis=0, concat_axis=1, tiled=True)  59.9 us
    all_to_all x1, waiting for transfers between devices, local(): lax.all_to_all(expert_out, 'tok', split_axis=1, concat_axis=0, tiled=True)  59 us
    dot_general x12, matrix products, loop_step(): jnp.einsum('hqd,hkd->hqk', query_heads, block[:heads_kv], preferred_eleme...  52.2 us
    convert_element_type x1, local copies, waits for them, and re-layouts, local(): expert_out = jnp.einsum('erf,efd->erd', hidden, w_down, preferred_element...  52.2 us
    select_n x2, local copies, waits for them, and re-layouts, local(): jnp.take(pool_heads, page_table[member_id], axis=1)  45.8 us
  transfers between devices with their start and end apart: 4, of which 4 were waited for; matrix products, arithmetic and copies ran while one was open for 8% of the time, Pallas kernels for 0%

profile of v1, /device:TPU:0, one launch (start us, length us, event | category | flops | bytes accessed | tf_op | source)
XLA Modules:
  0.0 975.0 jit_solution(13447912749562439598)
XLA Ops:
  27.2 23.2 %all-to-all-done = bf16[4,4,64,1024]{3,1,2,0:T(4,128)(2,1)} async-done(((bf16[4,4,64,1024]{3,1,2,0:T(4,128)(2,1)}), bf16[4,4,64,1024]{3,1,2,0:T(4,128)(2,1)}, u32[]{:S(2)}, u32[]{:S(2)}) %all-to-all-start) | async-done | bytes 2097184 | tf_op jit(solution)/shard_map/all_to_all | solution.py:128
  55.3 6.1 stack.14
  61.4 8.3 all-to-all-start.1
  82.1 5.2 fusion.125
  113.6 14.1 %all-gather.2.cloned.1.call-done = bf16[2048,2048]{1,0:T(8,128)(2,1)} async-done(((bf16[64,2048]{1,0:T(8,128)(2,1)}), bf16[2048,2048]{1,0:T(8,128)(2,1)}) %all-gather.2.cloned.1.call-update) | async-done | bytes 8388624 | tf_op jit(solution)/shard_map/all_gather | solution.py:164
  127.8 12.3 %copy.103 = bf16[2048,2048]{0,1:T(8,128)(2,1)} copy(bf16[2048,2048]{1,0:T(8,128)(2,1)} %all-gather.2.cloned.1.call-done) | data formatting | bytes 16777216 | tf_op jit(solution)/shard_map/all_gather | solution.py:164
  140.1 6.1 slice_bitcast_fusion.1
  146.2 144.3 %all-to-all-done.1 = bf16[32,4,64,1024]{3,2,1,0:T(8,128)(2,1)} async-done(((bf16[32,4,64,1024]{3,2,1,0:T(8,128)(2,1)}), bf16[32,4,64,1024]{3,2,1,0:T(8,128)(2,1)}, u32[]{:S(2)}, u32[]{:S(2)}) %all-to-all-start.1) | async-done | bytes 16777248 | tf_op jit(solution)/shard_map/all_to_all | solution.py:137
  290.4 43.1 %reshape_reshape.3 = bf16[128,64,16,64]{3,2,1,0:T(8,128)(2,1)} reshape(bf16[32,4,64,1024]{3,2,1,0:T(8,128)(2,1)} %all-to-all-done.1) | data formatting | bytes 33554432 | tf_op jit(solution)/shard_map/reshape;reshape | solution.py:145
  333.5 23.1 %copy.138 = bf16[128,64,16,64]{3,1,0,2:T(8,128)(2,1)} copy(bf16[128,64,16,64]{3,2,1,0:T(8,128)(2,1)} %reshape_reshape.3) | data formatting | bytes 33554432 | tf_op jit(solution)/shard_map/reshape;reshape | solution.py:145
  356.7 11.9 %gather_fusion.2 = bf16[64,16,64,64]{3,2,1,0:T(8,128)(2,1)} fusion(bf16[16,128,64,64]{3,2,1,0:T(8,128)(2,1)} %bitcast.229, s32[1024]{0:T(1024)S(1)} %pad_clamp_fusion.2), kind=kCustom, calls=%fused_computation.clone | custom fusion | bytes 16777472 | tf_op jit(solution)/shard_map/jit(_take)/gather | solution.py:150
  368.5 11.9 %gather_fusion.3 = bf16[64,16,64,64]{3,2,1,0:T(8,128)(2,1)} fusion(bf16[16,128,64,64]{3,2,1,0:T(8,128)(2,1)} %bitcast.230, s32[1024]{0:T(1024)S(1)} %pad_clamp_fusion.1), kind=kCustom, calls=%fused_computation.1.clone | custom fusion | bytes 16777472 | tf_op jit(solution)/shard_map/jit(_take)/gather | solution.py:150
  380.4 23.0 %select_bitcast_fusion = (bf16[16,64,64,64]{3,2,0,1:T(8,128)(2,1)}, bf16[16,64,64,64]{3,2,0,1:T(8,128)(2,1)}) fusion(bf16[64,16,64,64]{3,2,1,0:T(8,128)(2,1)} %gather_fusion.3, pred[64]{0:T(512)(128)(4,1)S(1)} %get-tuple-element.895, bf16[64,16,64,64]{3,2,1,0:T(8,128)(2,1)} %gather_fusion.2, pred[64]{0:T(512)(128)(4,1)S(1)} %get-tuple-element.873), kind=kLoop, calls=%fused_computation.92 | loop fusion | flops 8388608 | bytes 33554560 | tf_op jit(solution)/shard_map/jit(_take)/select_n | solution.py:150
  403.4 22.9 %copy.98 = bf16[16,64,64,64]{2,1,3,0:T(8,128)(2,1)} copy(bf16[16,64,64,64]{3,2,0,1:T(8,128)(2,1)} %get-tuple-element.902) | data formatting | bytes 16777216 | tf_op jit(solution)/shard_map/jit(_take)/select_n | solution.py:150
  426.3 22.6 %reshape.408 = bf16[16,4096,64]{1,2,0:T(8,128)(2,1)} reshape(bf16[16,64,64,64]{2,1,3,0:T(8,128)(2,1)} %copy.98) | data formatting | bytes 16777216 | tf_op jit(solution)/shard_map/reshape | solution.py:150
  448.9 60.4 %while.74 = (s32[]{:T(128)}, f32[8,192]{1,0:T(8,128)S(1)}, f32[8,192]{1,0:T(8,128)S(1)}, f32[8,192,64]{1,2,0:T(8,128)}, s32[4096]{0:T(1024)S(1)}, /*index=5*/bf1...) while((s32[]{:T(128)}, f32[8,192]{1,0:T(8,128)S(1)}, ...), condition=%wide.region_5.7_spmd.clone, body=%wide.region_2.6_spmd.clone.sunk | while | flops 423599616 | bytes 24100308 | solution.py:59
  449.1 5.2 fusion.178
  458.3 5.6 fusion.181
  464.2 5.2 fusion.178
  473.3 5.7 fusion.181
  479.3 5.2 fusion.178
  488.5 5.7 fusion.181
  494.4 5.2 fusion.178
  503.6 5.7 fusion.181
  509.3 27.0 %while.72 = (s32[]{:T(128)}, f32[8,192]{1,0:T(8,128)S(1)}, f32[8,192]{1,0:T(8,128)S(1)}, f32[8,192,64]{1,2,0:T(8,128)}, s32[2048]{0:T(1024)S(1)}, /*index=5*/bf1...) while((s32[]{:T(128)}, f32[8,192]{1,0:T(8,128)S(1)}, ...), condition=%wide.region_9.11_spmd.clone, body=%wide.region_6.10_spmd.clone.sunk | while | flops 423496704 | bytes 49266148 | solution.py:59
  517.2 5.7 fusion.168
  530.6 5.7 fusion.168
  537.0 22.9 %copy.106 = bf16[16,64,64,64]{2,1,3,0:T(8,128)(2,1)} copy(bf16[16,64,64,64]{3,2,0,1:T(8,128)(2,1)} %get-tuple-element.901) | data formatting | bytes 16777216 | tf_op jit(solution)/shard_map/jit(_take)/select_n | solution.py:150
  559.8 22.6 %reshape.412 = bf16[16,4096,64]{1,2,0:T(8,128)(2,1)} reshape(bf16[16,64,64,64]{2,1,3,0:T(8,128)(2,1)} %copy.106) | data formatting | bytes 16777216 | tf_op jit(solution)/shard_map/reshape | solution.py:150
  582.5 63.1 %while.75 = (s32[]{:T(128)}, f32[8,192]{1,0:T(8,128)S(1)}, f32[8,192]{1,0:T(8,128)S(1)}, f32[8,192,64]{1,2,0:T(8,128)}, s32[4096]{0:T(1024)}, /*index=5*/bf16[16...) while((s32[]{:T(128)}, f32[8,192]{1,0:T(8,128)S(1)}, ...), condition=%wide.region_13.15_spmd.clone, body=%wide.region_10.14_spmd.clone.sunk | while | flops 423599616 | bytes 24100308 | solution.py:59
  592.6 5.6 fusion.188
  608.2 5.7 fusion.188
  624.0 5.7 fusion.188
  639.8 5.7 fusion.188
  645.5 27.1 %while.73 = (s32[]{:T(128)}, f32[8,192]{1,0:T(8,128)S(1)}, f32[8,192]{1,0:T(8,128)S(1)}, f32[8,192,64]{1,2,0:T(8,128)}, s32[2048]{0:T(1024)S(1)}, /*index=5*/bf1...) while((s32[]{:T(128)}, f32[8,192]{1,0:T(8,128)S(1)}, ...), condition=%wide.region_17.19_spmd.clone, body=%wide.region_14.18_spmd.clone.sunk | while | flops 423496704 | bytes 49266148 | solution.py:59
  653.6 5.7 fusion.174
  667.0 5.7 fusion.174
  691.5 6.2 gather_fusion
  700.5 59.9 %all_to_all.28 = bf16[32,48,1536]{2,1,0:T(8,128)(2,1)S(1)} all-to-all(bf16[32,48,1536]{2,1,0:T(8,128)(2,1)S(1)} %select_select_fusion), channel_id=1, replica_groups=mesh['req'=4,'tok'=32] {'tok'}, dimensions={0} | all-to-all | bytes 9437184 | tf_op jit(solution)/shard_map/all_to_all | solution.py:211
  760.4 5.4 convolution_bitcast_fusion
  768.7 52.2 %copy.141 = bf16[1,1536,1536]{2,0,1:T(2,128)(2,1)} copy(bf16[1,1536,1536]{2,1,0:T(8,128)(2,1)S(1)} %fusion.78) | data formatting | bytes 9437184 | tf_op jit(solution)/shard_map/convert_element_type | solution.py:216
  821.4 32.0 %reduce.4 = bf16[1536,1536]{1,0:T(8,128)(2,1)} reduce(bf16[1536,1,1536]{2,1,0:T(2,128)(2,1)} %bitcast.231, bf16[]{:T(256)} %broadcast.487), dimensions={1}, to_apply=%bitcast.195.reduce_sub_computation | reduce | bytes 9437186
  853.4 8.2 reshape.483
  861.6 5.2 all-to-all-start.3
  867.5 59.0 %all-to-all-done.3 = bf16[32,2,36864]{2,1,0:T(2,128)(2,1)} async-done(((bf16[32,2,36864]{2,1,0:T(2,128)(2,1)}), bf16[32,2,36864]{2,1,0:T(2,128)(2,1)}, u32[]{:S(2)}, u32[]{:S(2)}) %all-to-all-start.3) | async-done | bytes 4718624 | tf_op jit(solution)/shard_map/all_to_all | solution.py:217
  926.5 20.2 %reshape.484 = bf16[1536,1,1536]{2,1,0:T(2,128)(2,1)} reshape(bf16[32,2,36864]{2,1,0:T(2,128)(2,1)} %all-to-all-done.3) | data formatting | bytes 9437184
  946.7 7.2 copy.139
  954.0 10.2 %gather_fusion.1 = bf16[1024,1536]{1,0:T(8,128)(2,1)} fusion(bf16[1536,1536]{1,0:T(8,128)(2,1)} %bitcast.228, s32[1024]{0:T(1024)S(1)} %broadcast_clamp_fusion), kind=kCustom, calls=%fused_computation.3 | custom fusion | bytes 6295552 | tf_op jit(solution)/shard_map/jit(_take)/gather | solution.py:218
  (249 shorter events, 181.1 us)
Async XLA Ops:
  7.2 753.2 %copy-start = (bf16[1,1536,1024]{2,1,0:T(8,128)(2,1)S(1)}, bf16[1,1536,1024]{2,1,0:T(8,128)(2,1)}, u32[]{:S(2)}) copy-start(bf16[1,1536,1024]{2,1,0:T(8,128)(2,1)} %param.36) | copy-start | bytes 9437188
  11.3 12.4 %copy-start.3 = (bf16[2,64,1536]{2,1,0:T(8,128)(2,1)S(1)}, bf16[2,64,1536]{2,1,0:T(8,128)(2,1)}, u32[]{:S(2)}) copy-start(bf16[2,64,1536]{2,1,0:T(8,128)(2,1)} %param.24) | copy-start | bytes 1179652
  11.3 12.6 %copy-start.10 = (f32[1536]{0:T(1024)S(1)}, f32[1536]{0:T(1024)}, u32[]{:S(2)}) copy-start(f32[1536]{0:T(1024)} %param.25) | copy-start | bytes 18436
  19.2 31.2 %all-to-all-start = ((bf16[4,4,64,1024]{3,1,2,0:T(4,128)(2,1)}), bf16[4,4,64,1024]{3,1,2,0:T(4,128)(2,1)}, u32[]{:S(2)}, u32[]{:S(2)}) async-start(bf16[4,4,64,1024]{3,1,2,0:T(4,128)(2,1)} %copy.94), calls=%async_computation | async-start | bytes 4194304 | tf_op jit(solution)/shard_map/all_to_all | solution.py:128
  23.8 104.0 %all-gather.2.cloned.1.call-start = ((), (), s32[]{:S(2)}) async-start(), calls=%async_computation.4 | async-start | bytes 8650752 | tf_op jit(solution)/shard_map/all_gather | solution.py:164
  61.4 229.0 %all-to-all-start.1 = ((bf16[32,4,64,1024]{3,2,1,0:T(8,128)(2,1)}), bf16[32,4,64,1024]{3,2,1,0:T(8,128)(2,1)}, u32[]{:S(2)}, u32[]{:S(2)}) async-start(bf16[32,4,64,1024]{3,2,1,0:T(8,128)(2,1)} %stack.14), calls=%async_computation.1 | async-start | bytes 33554432 | tf_op jit(solution)/shard_map/all_to_all | solution.py:137
  97.7 42.4 %copy-start.14 = (s32[2,512]{1,0:T(2,128)}, s32[2,512]{1,0:T(2,128)S(1)}, u32[]{:S(2)}) copy-start(s32[2,512]{1,0:T(2,128)S(1)} %fusion.111) | copy-start | bytes 12292
  98.5 41.6 %copy-start.11 = (s32[2,64,8]{1,2,0:T(8,128)}, s32[2,64,8]{1,2,0:T(8,128)S(1)}, u32[]{:S(2)}) copy-start(s32[2,64,8]{1,2,0:T(8,128)S(1)} %broadcast_multiply_fusion) | copy-start | bytes 12292
  98.7 0.6 copy-start.23
  99.4 40.7 %copy-start.19 = (s32[1024,1]{0,1:T(1,128)}, s32[1024,1]{0,1:T(1,128)S(1)}, u32[]{:S(2)}) copy-start(s32[1024,1]{0,1:T(1,128)S(1)} %compare_select_fusion) | copy-start | bytes 12292
  448.9 60.4 %copy-start.9 = (s32[2048]{0:T(1024)S(1)}, s32[2048]{0:T(1024)}, u32[]{:S(2)}) copy-start(s32[2048]{0:T(1024)} %iota_add_fusion.1) | copy-start | bytes 24580
  512.5 2.7 copy-start.1
  525.8 2.7 copy-start.1
  559.8 22.6 %copy-start.6 = (f32[8,192]{1,0:T(8,128)S(1)}, f32[8,192]{1,0:T(8,128)}, u32[]{:S(2)}) copy-start(f32[8,192]{1,0:T(8,128)} %custom-call.3) | copy-start | bytes 18436
  559.8 22.6 %copy-start.7 = (f32[8,192]{1,0:T(8,128)S(1)}, f32[8,192]{1,0:T(8,128)}, u32[]{:S(2)}) copy-start(f32[8,192]{1,0:T(8,128)} %custom-call.4) | copy-start | bytes 18436
  559.8 22.6 %copy-start.13 = (s32[64]{0:T(128)S(1)}, s32[64]{0:T(128)}, u32[]{:S(2)}) copy-start(s32[64]{0:T(128)} %get-tuple-element.1177) | copy-start | bytes 772
  582.5 63.1 %copy-start.8 = (s32[2048]{0:T(1024)S(1)}, s32[2048]{0:T(1024)}, u32[]{:S(2)}) copy-start(s32[2048]{0:T(1024)} %iota_add_fusion) | copy-start | bytes 24580
  648.8 2.7 copy-start.2
  662.2 2.7 copy-start.2
  672.7 14.5 %copy-start.4 = (bf16[2,64,1536]{2,1,0:T(8,128)(2,1)S(1)}, bf16[2,64,1536]{2,1,0:T(8,128)(2,1)}, u32[]{:S(2)}) copy-start(bf16[2,64,1536]{2,1,0:T(8,128)(2,1)} %param.24) | copy-start | bytes 1179652
  675.6 15.0 %copy-start.21 = (f32[1536]{0:T(1024)S(1)}, f32[1536]{0:T(1024)}, u32[]{:S(2)}) copy-start(f32[1536]{0:T(1024)} %param.33) | copy-start | bytes 18436
  678.5 12.9 %copy-start.16 = (s32[2048]{0:T(1024)S(1)}, s32[2048]{0:T(1024)}, u32[]{:S(2)}) copy-start(s32[2048]{0:T(1024)} %pad_clamp_fusion) | copy-start | bytes 24580
  687.1 3.4 copy-start.5
  691.5 6.2 copy-start.17
  691.5 6.2 copy-start.18
  760.4 5.4 copy-start.25
  861.6 5.3 copy-start.15
  861.6 5.4 copy-start.12
  861.6 5.5 copy-start.24
  861.6 5.8 copy-start.22
  861.6 5.9 copy-start.20
  861.6 64.9 %all-to-all-start.3 = ((bf16[32,2,36864]{2,1,0:T(2,128)(2,1)}), bf16[32,2,36864]{2,1,0:T(2,128)(2,1)}, u32[]{:S(2)}, u32[]{:S(2)}) async-start(bf16[32,2,36864]{2,1,0:T(2,128)(2,1)} %reshape.483), calls=%async_computation.3 | async-start | bytes 9437184 | tf_op jit(solution)/shard_map/all_to_all | solution.py:217
Sparse Core Ops, SparseCore 0:
  27.4 100.2 all-gather.1
